TPU v7x, 256 devices: a whole 4x4x8 slice. The times are simulated.
256 devices in a mesh: tile: 32 (over z_lo, y, core), lev: 8 (over x, z_hi).
Axes of the slice: x: 4, y: 4, z: 8 (z_hi: 2, z_lo: 4; z = z_hi * 4 + z_lo), core: 2. Of those that a mesh axis runs over, the one named last changes fastest.
Arguments:
- costate_ending_fields: float32 [4, 16, 32, 32, 128], P(None, 'lev', 'tile'), may hold values from -6 to 6
- costate_ending_elevation: float32 [32, 32, 128], P('tile'), may hold values from -6 to 6
- upstream_transport_coefficient: float32 [16, 32, 32, 128], P('lev', 'tile'), may hold values from 0.05 to 0.45
- eastward_spread_coefficient: float32 [32, 32, 128], P('tile'), may hold values from 0.02 to 0.2
- interface_blending_coefficient: float32 [16, 32, 32, 128], P('lev', 'tile'), may hold values from 0.02 to 0.3
- thickness_sensitivity: float32 [4, 16, 32, 32, 128], P(None, 'lev', 'tile'), may hold values from -1.75 to 1.75
- layer_velocity_factor: float32 [16, 32, 32, 128], P('lev', 'tile'), may hold values from 0.02 to 0.1
- western_join_turned: int32 [32], replicated, may hold values from 0 to 1
- predicted_thermal_skin: float32 [32, 32, 128], P('tile'), may hold values from -6 to 6
- predicted_elevation: float32 [32, 32, 128], P('tile'), may hold values from -6 to 6
- measured_quantity: float32 [8, 32, 32, 512], P('lev', 'tile'), may hold values from -6 to 6
- measurement_precision: float32 [8, 32, 32, 512], P('lev', 'tile'), may hold values from 0.05 to 0.3
- measurement_sort: int32 [8, 32, 32, 512], P('lev', 'tile'), may hold values from 0 to 1
- sampled_location: int32 [8, 32, 32, 512], P('lev', 'tile'), may hold values from 0 to 4095
- active_entry_numbers: int32 [8, 32, 32], P('lev', 'tile'), may hold values from 0 to 512, as said below
Outputs:
- adj_state_start: float32 [4, 16, 32, 32, 128], P(None, 'lev', 'tile')
- adj_height_start: float32 [32, 32, 128], P('tile')
Inputs may be any that keep to these rules, and one draw needn't show every extreme that they name: `western_join_turned`: 1 means a rotated seam. `active_entry_numbers`: slots at or above the count carry no record; in every draw some destination tile has all 512 slots live from every source tile in every level group.
All inputs are finite; a program needn't handle non-finite values.
Results may differ from a plain program's by a relative error of at most 0.0003.
Values sent between devices are 32-bit elements; how exact they have to be, the bound alone decides.
No kernel may reach another device: no remote copies, remote signals or barrier semaphores. Data moves between devices by JAX's collectives and lax.ppermute only.
A program may use at most 64 MiB of HBM per device.

v0:
```python
import jax
import jax.numpy as jnp
from jax import lax
from jax.sharding import PartitionSpec as P

OUT_SIGN = (1.0, 1.0, -1.0, 1.0)
SEAM_ORDER = (0, 1, 3, 2)


def shifted(value, axis, steps):
    count = lax.axis_size(axis)
    pairs = [(source, (source + steps) % count) for source in range(count)]
    return lax.ppermute(value, axis, pairs)


def from_behind(block, axis, distance):
    devices = range(lax.axis_size(axis))
    route = [(i - distance, i) for i in devices if i - distance in devices]
    return lax.ppermute(block, axis, route)


def adjoint_step(lam_state, lam_height, flow_l, diff_l, mix_l, stretch_l, weight_l, rotated):
    scaled = flow_l[None] * lam_state
    advect = jnp.concatenate([scaled[..., 1:], jnp.zeros_like(scaled[..., :1])], axis=-1) - scaled
    edge = scaled[..., 0]
    sign = jnp.array(OUT_SIGN, jnp.float32)[:, None, None]
    order = jnp.array(SEAM_ORDER, jnp.int32)
    outgoing = jnp.where(rotated, sign * edge[order][..., ::-1], edge)
    incoming = shifted(outgoing, "tile", -1)
    advect = advect.at[..., -1].add(incoming)
    next_row = jnp.concatenate(
        [lam_state[..., 1:, :], jnp.zeros_like(lam_state[..., :1, :])], axis=-2
    )
    face_y = diff_l[None, None] * (next_row - lam_state)
    mix_row = face_y - jnp.concatenate(
        [jnp.zeros_like(face_y[..., :1, :]), face_y[..., :-1, :]], axis=-2
    )
    below = from_behind(lam_state[:, :1], "lev", -1)
    lower = jnp.concatenate([lam_state[:, 1:], below], axis=1)
    face_z = mix_l[None] * (lower - lam_state)
    above = from_behind(face_z[:, -1:], "lev", 1)
    mix_col = face_z - jnp.concatenate([above, face_z[:, :-1]], axis=1)
    new_state = lam_state + advect + mix_row + mix_col
    new_state = new_state.at[2].add(weight_l * lam_height[None])
    column_part = jnp.sum(stretch_l * lam_state, axis=(0, 1))
    new_height = lam_height + lax.psum(column_part, "lev")
    return (new_state, new_height)


def per_device(
    costate_ending_fields,
    costate_ending_elevation,
    upstream_transport_coefficient,
    eastward_spread_coefficient,
    interface_blending_coefficient,
    thickness_sensitivity,
    layer_velocity_factor,
    western_join_turned,
    predicted_thermal_skin,
    predicted_elevation,
    measured_quantity,
    measurement_precision,
    measurement_sort,
    sampled_location,
    active_entry_numbers,
):
    lev_dev = costate_ending_fields.shape[1]
    rows = costate_ending_fields.shape[3]
    cols = costate_ending_fields.shape[4]
    slots = measured_quantity.shape[3]
    lev_index = lax.axis_index("lev")
    tile_index = lax.axis_index("tile")
    level_total = lev_dev * lax.axis_size("lev")
    global_level = lev_index * lev_dev + jnp.arange(lev_dev, dtype=jnp.int32)
    mix_l = (
        interface_blending_coefficient[:, 0]
        * (global_level < level_total - 1).astype(jnp.float32)[:, None, None]
    )
    row_mask = (jnp.arange(rows) < rows - 1).astype(jnp.float32)[:, None]
    diff_l = eastward_spread_coefficient[0] * row_mask
    flow_l = upstream_transport_coefficient[:, 0]
    stretch_l = thickness_sensitivity[:, :, 0]
    weight_l = layer_velocity_factor[:, 0]
    rotated = western_join_turned[tile_index] == 1
    live = jnp.arange(slots, dtype=jnp.int32)[None, :] < active_entry_numbers[0, 0][:, None]
    packet = jnp.stack(
        [
            measured_quantity[0, 0],
            jnp.where(live, measurement_precision[0, 0], 0.0),
            measurement_sort[0, 0].astype(jnp.float32),
            sampled_location[0, 0].astype(jnp.float32),
        ]
    )
    arrived = lax.all_to_all(packet, "tile", split_axis=1, concat_axis=1, tiled=True)
    record_kind = arrived[2].astype(jnp.int32)
    mesh_point = arrived[3].astype(jnp.int32)
    marine_dynamics = jnp.where(
        record_kind == 0,
        predicted_thermal_skin.reshape(-1)[mesh_point],
        predicted_elevation.reshape(-1)[mesh_point],
    )
    misfit = arrived[1] * (marine_dynamics - arrived[0])
    target = (record_kind * (rows * cols) + mesh_point).reshape(-1)
    maps = (
        jnp.zeros((2 * rows * cols,), jnp.float32)
        .at[target]
        .add(misfit.reshape(-1))
        .reshape(2, rows, cols)
    )
    maps = lax.psum(maps, "lev")
    lam_state = costate_ending_fields[:, :, 0]
    lam_state = lam_state.at[0, 0].add(jnp.where(lev_index == 0, maps[0], 0.0))
    lam_height = costate_ending_elevation[0] + maps[1]
    for turn in range(2):
        lam_state, lam_height = adjoint_step(
            lam_state, lam_height, flow_l, diff_l, mix_l, stretch_l, weight_l, rotated
        )
    return (lam_state[:, :, None], lam_height[None])


def solution(mesh):
    placed = (
        P(None, "lev", "tile", None, None),
        P("tile", None, None),
        P("lev", "tile", None, None),
        P("tile", None, None),
        P("lev", "tile", None, None),
        P(None, "lev", "tile", None, None),
        P("lev", "tile", None, None),
        P(),
        P("tile", None, None),
        P("tile", None, None),
        P("lev", "tile", None, None),
        P("lev", "tile", None, None),
        P("lev", "tile", None, None),
        P("lev", "tile", None, None),
        P("lev", "tile", None),
    )
    return jax.shard_map(
        per_device,
        mesh=mesh,
        in_specs=placed,
        out_specs=(P(None, "lev", "tile", None, None), P("tile", None, None)),
        check_vma=False,
    )
```

profile of v0, /device:TPU:38, one launch (start us, length us, event | category | flops | bytes accessed | tf_op | source)
XLA Modules:
  0.0 480.6 jit_solution(5255978705896090962)
XLA Ops:
  0.7 0.9 stack_squeeze.3
  1.6 0.8 copy-done.13
  2.5 0.8 copy-done.14
  3.5 1.0 pad_maximum_fusion
  4.5 8.9 %all-to-all-start = ((f32[4,32,512]{2,0,1:T(4,128)}), f32[4,32,512]{2,0,1:T(4,128)S(1)}, u32[]{:S(2)}, u32[]{:S(2)}) async-start(f32[4,32,512]{2,0,1:T(4,128)} %pad_maximum_fusion), calls=%async_computation | async-start | bytes 524288 | tf_op jit(solution)/shard_map/all_to_all | solution.py:94
  13.5 0.3 copy.105
  14.1 0.6 copy-done.18
  14.8 0.6 copy-done.17
  15.7 0.6 copy-done.15
  16.4 0.6 copy-done.16
  17.2 0.6 copy-done.23
  17.9 0.6 dynamic_slice.3
  19.1 4.3 all-to-all-done
  23.5 0.3 compare_reduce_fusion
  23.9 90.5 %gather_fusion.1 = f32[16384]{0:T(1024)S(1)} fusion(f32[4096]{0:T(1024)S(1)} %bitcast.73, s32[16384]{0:T(1024)S(1)} %broadcast_clamp_fusion), kind=kCustom, calls=%fused_computation.1 | custom fusion | bytes 196608 | tf_op jit(solution)/shard_map/gather | solution.py:100
  114.5 90.5 %gather_fusion = f32[16384]{0:T(1024)S(1)} fusion(f32[4096]{0:T(1024)S(1)} %bitcast.74, s32[16384]{0:T(1024)S(1)} %broadcast_clamp_fusion), kind=kCustom, calls=%fused_computation | custom fusion | bytes 196608 | tf_op jit(solution)/shard_map/gather | solution.py:99
  205.4 85.8 %scatter_custom_fusion = f32[8192]{0:T(1024)S(1)} fusion(s32[16384]{0:T(1024)S(1)} %bitcast.86, f32[16384]{0:T(1024)S(1)} %subtract_multiply_fusion.2, f32[]{:T(128)} %constant.154.clone.1), kind=kCustom, calls=%fused_computation.50 | custom fusion | flops 16384 | bytes 32772 | tf_op jit(solution)/shard_map/scatter-add | solution.py:107
  291.4 54.0 %psum.21 = f32[2,32,128]{1,2,0:T(8,128)S(1)} all-reduce(f32[2,32,128]{1,2,0:T(8,128)S(1)} %copy.109), channel_id=1, replica_groups=mesh['tile'=32,'lev'=8] {'lev'}, use_global_device_ids=true, to_apply=%region_1.2 | all-reduce | flops 8192 | bytes 65536 | tf_op jit(solution)/shard_map/psum | solution.py:110
  345.4 1.6 scatter-add.25
  347.1 0.4 fusion.19
  347.5 1.9 collective-permute-start.1
  349.4 0.6 slice.246
  350.0 12.1 %collective-permute-done.1 = f32[4,1,32,128]{2,1,0,3:T(1,128)S(1)} collective-permute-done((f32[4,1,32,128]{2,1,0,3:T(1,128)S(1)}, f32[4,1,32,128]{2,1,0,3:T(1,128)S(1)}, u32[]{:S(2)}, u32[]{:S(2)}) %collective-permute-start.1) | collective-permute-done | bytes 65568 | tf_op jit(solution)/shard_map/ppermute | solution.py:19
  362.1 1.2 broadcast_multiply_fusion.1
  363.4 0.6 gather_fusion.2
  364.1 0.7 copy-done.20
  364.8 0.3 pad_subtract_fusion.1
  365.2 0.4 fusion.18
  365.6 1.9 collective-permute-start.2
  367.5 17.1 %collective-permute-done.2 = f32[4,1,32,128]{2,1,0,3:T(1,128)S(1)} collective-permute-done((f32[4,1,32,128]{2,1,0,3:T(1,128)S(1)}, f32[4,1,32,128]{2,1,0,3:T(1,128)S(1)}, u32[]{:S(2)}, u32[]{:S(2)}) %collective-permute-start.2) | collective-permute-done | bytes 65568 | tf_op jit(solution)/shard_map/ppermute | solution.py:19
  384.7 1.2 fusion.1
  386.0 1.1 fusion.17
  387.1 2.6 collective-permute-start.4
  389.7 0.3 copy.116
  390.1 0.6 slice.257
  390.7 16.0 %collective-permute-done.4 = f32[4,1,32,128]{2,1,0,3:T(1,128)S(1)} collective-permute-done((f32[4,1,32,128]{2,1,0,3:T(1,128)S(1)}, f32[4,1,32,128]{2,1,0,3:T(1,128)S(1)}, u32[]{:S(2)}, u32[]{:S(2)}) %collective-permute-start.4) | collective-permute-done | bytes 65568 | tf_op jit(solution)/shard_map/ppermute | solution.py:19
  406.7 0.7 copy-done.9
  407.4 3.7 fusion.5
  411.1 0.6 gather_fusion.3
  411.9 0.3 pad_subtract_fusion
  412.3 0.4 fusion.16
  412.7 0.4 copy-done.7
  413.1 48.6 %all-reduce.6 = (f32[32,128]{0,1:T(8,128)S(1)}, f32[32,128]{0,1:T(8,128)S(1)}) all-reduce(f32[32,128]{0,1:T(8,128)S(1)} %copy-done.8, f32[32,128]{0,1:T(8,128)S(1)} %copy-done.7), channel_id=1, replica_groups=mesh['tile'=32,'lev'=8] {'lev'}, use_global_device_ids=true, to_apply=%region_3.4 | all-reduce | flops 8192 | bytes 65536 | tf_op jit(solution)/shard_map/psum | solution.py:46
  461.8 0.7 copy.119
  462.5 7.3 %collective-permute-start.5 = (f32[4,1,32,128]{2,1,0,3:T(1,128)S(1)}, f32[4,1,32,128]{2,1,0,3:T(1,128)S(1)}, u32[]{:S(2)}, u32[]{:S(2)}) collective-permute-start(f32[4,1,32,128]{2,1,0,3:T(1,128)S(1)} %get-tuple-element.81), channel_id=1, source_target_pairs={{0,1},{1,2},{2,3},{3,4},{4,5},{5,6},{6,7},{8,9},{9,10},{10,11},{11... | collective-permute-start | bytes 196616 | tf_op jit(solution)/shard_map/ppermute | solution.py:19
  469.9 8.4 %collective-permute-done.5 = f32[4,1,32,128]{2,1,0,3:T(1,128)S(1)} collective-permute-done((f32[4,1,32,128]{2,1,0,3:T(1,128)S(1)}, f32[4,1,32,128]{2,1,0,3:T(1,128)S(1)}, u32[]{:S(2)}, u32[]{:S(2)}) %collective-permute-start.5) | collective-permute-done | bytes 65568 | tf_op jit(solution)/shard_map/ppermute | solution.py:19
  478.2 1.2 fusion.3
  479.6 1.0 copy.118
  (82 shorter events, 2.6 us)
Async XLA Ops:
  0.6 23.3 %copy-start = (f32[1,32,128]{2,1,0:T(8,128)S(1)}, f32[1,32,128]{2,1,0:T(8,128)}, u32[]{:S(2)}) copy-start(f32[1,32,128]{2,1,0:T(8,128)} %param.38) | copy-start | bytes 49156
  0.6 0.9 copy-start.12
  1.6 0.8 copy-start.13
  2.4 0.8 copy-start.14
  2.4 0.8 copy-start.21
  4.5 9.0 %copy-start.19 = (f32[1,32,128]{2,1,0:T(8,128)S(1)}, f32[1,32,128]{2,1,0:T(8,128)}, u32[]{:S(2)}) copy-start(f32[1,32,128]{2,1,0:T(8,128)} %param.32) | copy-start | bytes 49156
  4.5 9.0 %copy-start.10 = (f32[4,2,1,32,128]{4,3,2,1,0:T(8,128)S(1)}, f32[4,2,1,32,128]{4,3,2,1,0:T(8,128)}, u32[]{:S(2)}) copy-start(f32[4,2,1,32,128]{4,3,2,1,0:T(8,128)} %param.29) | copy-start | bytes 393220
  4.5 19.0 %all-to-all-start = ((f32[4,32,512]{2,0,1:T(4,128)}), f32[4,32,512]{2,0,1:T(4,128)S(1)}, u32[]{:S(2)}, u32[]{:S(2)}) async-start(f32[4,32,512]{2,0,1:T(4,128)} %pad_maximum_fusion), calls=%async_computation | async-start | bytes 524288 | tf_op jit(solution)/shard_map/all_to_all | solution.py:94
  14.0 0.7 copy-start.18
  14.7 0.8 copy-start.17
  15.6 0.8 copy-start.15
  16.3 0.8 copy-start.16
  17.1 345.1 %copy-start.2 = (f32[2,32,128]{1,0,2:T(2,128)}, f32[2,32,128]{1,0,2:T(2,128)S(1)}, u32[]{:S(2)}) copy-start(f32[2,32,128]{1,0,2:T(2,128)S(1)} %copy.111) | copy-start | bytes 98308
  17.2 0.7 copy-start.23
  18.4 0.7 copy-start.22
  23.9 90.6 %copy-start.1 = (f32[1,32,128]{2,1,0:T(8,128)S(1)}, f32[1,32,128]{2,1,0:T(8,128)}, u32[]{:S(2)}) copy-start(f32[1,32,128]{2,1,0:T(8,128)} %param.37) | copy-start | bytes 49156
  347.5 14.7 %collective-permute-start.1 = (f32[4,1,32,128]{2,1,0,3:T(1,128)S(1)}, f32[4,1,32,128]{2,1,0,3:T(1,128)S(1)}, u32[]{:S(2)}, u32[]{:S(2)}) collective-permute-start(f32[4,1,32,128]{2,1,0,3:T(1,128)S(1)} %get-tuple-element.91), channel_id=1, source_target_pairs={{1,0},{2,1},{3,2},{4,3},{5,4},{6,5},{7,6},{9,8},{10,9},{11,10},{12... | collective-permute-start | bytes 196616 | tf_op jit(solution)/shard_map/ppermute | solution.py:19
  349.4 36.4 %copy-start.5 = (f32[32,128]{0,1:T(8,128)}, f32[32,128]{0,1:T(8,128)S(1)}, u32[]{:S(2)}) copy-start(f32[32,128]{0,1:T(8,128)S(1)} %fusion.9) | copy-start | bytes 49156
  364.1 0.7 copy-start.20
  364.8 2.7 collective-permute-start
  365.6 19.1 %collective-permute-start.2 = (f32[4,1,32,128]{2,1,0,3:T(1,128)S(1)}, f32[4,1,32,128]{2,1,0,3:T(1,128)S(1)}, u32[]{:S(2)}, u32[]{:S(2)}) collective-permute-start(f32[4,1,32,128]{2,1,0,3:T(1,128)S(1)} %get-tuple-element.88), channel_id=1, source_target_pairs={{0,1},{1,2},{2,3},{3,4},{4,5},{5,6},{6,7},{8,9},{9,10},{10,11},{11... | collective-permute-start | bytes 196616 | tf_op jit(solution)/shard_map/ppermute | solution.py:19
  386.0 3.7 copy-start.11
  387.1 19.6 %collective-permute-start.4 = (f32[4,1,32,128]{2,1,0,3:T(1,128)S(1)}, f32[4,1,32,128]{2,1,0,3:T(1,128)S(1)}, u32[]{:S(2)}, u32[]{:S(2)}) collective-permute-start(f32[4,1,32,128]{2,1,0,3:T(1,128)S(1)} %get-tuple-element.84), channel_id=1, source_target_pairs={{1,0},{2,1},{3,2},{4,3},{5,4},{6,5},{7,6},{9,8},{10,9},{11,10},{12... | collective-permute-start | bytes 196616 | tf_op jit(solution)/shard_map/ppermute | solution.py:19
  390.1 17.3 %copy-start.3 = (f32[2,32,128]{1,0,2:T(2,128)S(1)}, f32[2,32,128]{1,0,2:T(2,128)}, u32[]{:S(2)}) copy-start(f32[2,32,128]{1,0,2:T(2,128)} %copy-done.2) | copy-start | bytes 98308
  390.1 17.3 %copy-start.4 = (f32[4,1,32,128]{2,1,0,3:T(1,128)S(1)}, f32[4,1,32,128]{2,1,0,3:T(1,128)}, u32[]{:S(2)}) copy-start(f32[4,1,32,128]{2,1,0,3:T(1,128)} %get-tuple-element.83) | copy-start | bytes 196612
  406.7 0.7 copy-start.9
  411.9 58.0 %collective-permute-start.3 = (f32[4,2,32]{2,1,0:T(2,128)S(1)}, f32[4,2,32]{2,1,0:T(2,128)S(1)}, u32[]{:S(2)}, u32[]{:S(2)}) collective-permute-start(f32[4,2,32]{2,1,0:T(2,128)S(1)} %multiply_select_fusion), channel_id=1, source_target_pairs={{0,248},{8,0},{16,8},{24,16},{32,24},{40,32},{48,40},{56,48},{64,5... | collective-permute-start | bytes 3080 | tf_op jit(solution)/shard_map/ppermute | solution.py:13
  412.3 0.8 copy-start.7
  412.3 0.9 copy-start.8
  413.1 48.7 %copy-start.6 = (f32[32,128]{0,1:T(8,128)S(1)}, f32[32,128]{0,1:T(8,128)}, u32[]{:S(2)}) copy-start(f32[32,128]{0,1:T(8,128)} %copy-done.5) | copy-start | bytes 49156
  462.5 15.7 %collective-permute-start.5 = (f32[4,1,32,128]{2,1,0,3:T(1,128)S(1)}, f32[4,1,32,128]{2,1,0,3:T(1,128)S(1)}, u32[]{:S(2)}, u32[]{:S(2)}) collective-permute-start(f32[4,1,32,128]{2,1,0,3:T(1,128)S(1)} %get-tuple-element.81), channel_id=1, source_target_pairs={{0,1},{1,2},{2,3},{3,4},{4,5},{5,6},{6,7},{8,9},{9,10},{10,11},{11... | collective-permute-start | bytes 196616 | tf_op jit(solution)/shard_map/ppermute | solution.py:19
where the time goes:
time: 481 us
  local copies, waits for them, and re-layouts  199 us (41%)
  blocking collectives  103 us (21%)
  other arithmetic  96.2 us (20%)
  waiting for transfers between devices  57.9 us (12%)
  starting transfers between devices  22.7 us (5%)
    gather x1, local copies, waits for them, and re-layouts, per_device(): predicted_elevation.reshape(-1)[mesh_point]  90.5 us
    gather x1, local copies, waits for them, and re-layouts, per_device(): predicted_thermal_skin.reshape(-1)[mesh_point]  90.5 us
    scatter-add x1, other arithmetic, per_device(): maps = jnp.zeros((2 * rows * cols,), jnp.float32).at[target].add(misfit.r...  85.8 us
    psum x1, blocking collectives, per_device(): maps = lax.psum(maps, 'lev')  54 us
    ppermute x4, waiting for transfers between devices, from_behind(): return lax.ppermute(block, axis, route)  53.6 us
    psum x1, blocking collectives, adjoint_step(): new_height = lam_height + lax.psum(column_part, 'lev')  48.6 us
    ppermute x4, starting transfers between devices, from_behind(): return lax.ppermute(block, axis, route)  13.7 us
  transfers between devices with their start and end apart: 7, of which 5 were waited for; matrix products, arithmetic and copies ran while one was open for 1% of the time, Pallas kernels for 0%

commit v1 on v0

--- a/solution.py
+++ b/solution.py
@@ -43,7 +43,8 @@
     new_state = lam_state + advect + mix_row + mix_col
     new_state = new_state.at[2].add(weight_l * lam_height[None])
     column_part = jnp.sum(stretch_l * lam_state, axis=(0, 1))
-    new_height = lam_height + lax.psum(column_part, "lev")
+    close_shelves_up = lambda row_data, chip_axis: lax.all_gather(row_data, chip_axis).sum(axis=0)
+    new_height = lam_height + close_shelves_up(column_part, "lev")
     return (new_state, new_height)
 
 

time: 481 us -> 519 us (1.079)
  blocking collectives: 103 us -> 137 us
    all_gather x0 -> x2, blocking collectives: none -> 87.2 us  [adjoint_step(): lax.all_gather(row_data, chip_axis).sum(axis=0)]
    psum x1 -> x0, blocking collectives: 48.6 us -> none  [adjoint_step(): new_height = lam_height + lax.psum(column_part, 'lev')]
where the time goes in v1:
time: 519 us; the launch traced here: 517 us
  local copies, waits for them, and re-layouts  200 us (39%)
  blocking collectives  137 us (26%)
  other arithmetic  98.3 us (19%)
  waiting for transfers between devices  58.8 us (11%)
  starting transfers between devices  21.4 us (4%)
    gather x1, local copies, waits for them, and re-layouts, per_device(): predicted_elevation.reshape(-1)[mesh_point]  90.5 us
    gather x1, local copies, waits for them, and re-layouts, per_device(): predicted_thermal_skin.reshape(-1)[mesh_point]  90.5 us
    all_gather x2, blocking collectives, adjoint_step(): lax.all_gather(row_data, chip_axis).sum(axis=0)  87.2 us
    scatter-add x1, other arithmetic, per_device(): maps = jnp.zeros((2 * rows * cols,), jnp.float32).at[target].add(misfit.r...  85.8 us
    ppermute x4, waiting for transfers between devices, from_behind(): return lax.ppermute(block, axis, route)  54.3 us
    psum x1, blocking collectives, per_device(): maps = lax.psum(maps, 'lev')  49.7 us
    ppermute x4, starting transfers between devices, from_behind(): return lax.ppermute(block, axis, route)  12.5 us
  transfers between devices with their start and end apart: 7, of which 5 were waited for; matrix products, arithmetic and copies ran while one was open for 1% of the time, Pallas kernels for 0%

profile of v1, /device:TPU:38, one launch (start us, length us, event | category | flops | bytes accessed | tf_op | source)
XLA Modules:
  0.0 517.0 jit_solution(357013659498480095)
XLA Ops:
  0.7 0.9 stack_squeeze.3
  1.6 0.8 copy-done.14
  2.5 0.8 copy-done.15
  3.5 1.0 pad_maximum_fusion
  4.5 8.9 %all-to-all-start = ((f32[4,32,512]{2,0,1:T(4,128)}), f32[4,32,512]{2,0,1:T(4,128)S(1)}, u32[]{:S(2)}, u32[]{:S(2)}) async-start(f32[4,32,512]{2,0,1:T(4,128)} %pad_maximum_fusion), calls=%async_computation | async-start | bytes 524288 | tf_op jit(solution)/shard_map/all_to_all | solution.py:95
  13.6 0.6 copy-done.20
  14.5 0.6 copy-done.18
  15.2 0.6 copy-done.19
  16.0 0.3 copy.130
  16.4 0.6 copy-done.25
  17.0 0.6 dynamic_slice.3
  18.3 0.6 pad_clamp_fusion
  18.9 4.5 all-to-all-done
  23.9 90.5 %gather_fusion.1 = f32[16384]{0:T(1024)S(1)} fusion(f32[4096]{0:T(1024)S(1)} %bitcast.82, s32[16384]{0:T(1024)S(1)} %broadcast_clamp_fusion), kind=kCustom, calls=%fused_computation.1 | custom fusion | bytes 196608 | tf_op jit(solution)/shard_map/gather | solution.py:101
  114.5 90.5 %gather_fusion = f32[16384]{0:T(1024)S(1)} fusion(f32[4096]{0:T(1024)S(1)} %bitcast.83, s32[16384]{0:T(1024)S(1)} %broadcast_clamp_fusion), kind=kCustom, calls=%fused_computation | custom fusion | bytes 196608 | tf_op jit(solution)/shard_map/gather | solution.py:100
  205.4 85.8 %scatter_custom_fusion = f32[8192]{0:T(1024)S(1)} fusion(s32[16384]{0:T(1024)S(1)} %bitcast.96, f32[16384]{0:T(1024)S(1)} %subtract_multiply_fusion.2, f32[]{:T(128)} %constant.154.clone.1), kind=kCustom, calls=%fused_computation.50 | custom fusion | flops 16384 | bytes 32772 | tf_op jit(solution)/shard_map/scatter-add | solution.py:108
  291.2 49.7 %psum.7 = f32[2,32,128]{2,1,0:T(8,128)S(1)} all-reduce(f32[2,32,128]{2,1,0:T(8,128)S(1)} %bitcast.94), channel_id=1, replica_groups=mesh['tile'=32,'lev'=8] {'lev'}, use_global_device_ids=true, to_apply=%region_1.2 | all-reduce | flops 8192 | bytes 65536 | tf_op jit(solution)/shard_map/psum | solution.py:111
  341.1 1.6 scatter-add.25
  342.7 0.4 fusion.20
  343.1 1.9 collective-permute-start.1
  345.1 0.6 slice.246
  345.8 12.0 %collective-permute-done.1 = f32[4,1,32,128]{2,1,0,3:T(1,128)S(1)} collective-permute-done((f32[4,1,32,128]{2,1,0,3:T(1,128)S(1)}, f32[4,1,32,128]{2,1,0,3:T(1,128)S(1)}, u32[]{:S(2)}, u32[]{:S(2)}) %collective-permute-start.1) | collective-permute-done | bytes 65568 | tf_op jit(solution)/shard_map/ppermute | solution.py:19
  357.8 0.7 copy-done.8
  358.5 2.2 broadcast_multiply_fusion.1
  360.7 0.7 gather_fusion.2
  361.5 0.7 copy-done.22
  362.6 0.4 fusion.19
  363.0 1.9 collective-permute-start.2
  365.0 18.1 %collective-permute-done.2 = f32[4,1,32,128]{2,1,0,3:T(1,128)S(1)} collective-permute-done((f32[4,1,32,128]{2,1,0,3:T(1,128)S(1)}, f32[4,1,32,128]{2,1,0,3:T(1,128)S(1)}, u32[]{:S(2)}, u32[]{:S(2)}) %collective-permute-start.2) | collective-permute-done | bytes 65568 | tf_op jit(solution)/shard_map/ppermute | solution.py:19
  383.0 1.2 fusion.1
  384.4 1.1 fusion.18
  385.5 2.9 collective-permute-start.4
  388.4 0.3 copy.139
  388.8 0.6 slice.257
  389.4 15.3 %collective-permute-done.4 = f32[4,1,32,128]{2,1,0,3:T(1,128)S(1)} collective-permute-done((f32[4,1,32,128]{2,1,0,3:T(1,128)S(1)}, f32[4,1,32,128]{2,1,0,3:T(1,128)S(1)}, u32[]{:S(2)}, u32[]{:S(2)}) %collective-permute-start.4) | collective-permute-done | bytes 65568 | tf_op jit(solution)/shard_map/ppermute | solution.py:19
  404.7 0.7 copy-done.7
  405.4 3.7 fusion.5
  409.2 0.8 copy-done.6
  410.0 0.7 gather_fusion.3
  411.0 43.0 %all-gather = f32[256,128]{1,0:T(8,128)S(1)} all-gather(f32[32,128]{1,0:T(8,128)S(1)} %copy.140), channel_id=2, replica_groups=mesh['tile'=32,'lev'=8] {'lev'}, dimensions={0}, use_global_device_ids=true | all-gather | bytes 147456 | tf_op jit(solution)/shard_map/all_gather | solution.py:46
  454.0 44.2 %all-gather.1 = f32[256,128]{1,0:T(8,128)S(1)} all-gather(f32[32,128]{1,0:T(8,128)S(1)} %copy.143), channel_id=3, replica_groups=mesh['tile'=32,'lev'=8] {'lev'}, dimensions={0}, use_global_device_ids=true | all-gather | bytes 147456 | tf_op jit(solution)/shard_map/all_gather | solution.py:46
  498.2 0.3 pad_subtract_fusion
  498.6 0.4 fusion.17
  499.3 0.6 bitcast_add_fusion
  500.0 5.7 %collective-permute-start.5 = (f32[4,1,32,128]{2,1,0,3:T(1,128)S(1)}, f32[4,1,32,128]{2,1,0,3:T(1,128)S(1)}, u32[]{:S(2)}, u32[]{:S(2)}) collective-permute-start(f32[4,1,32,128]{2,1,0,3:T(1,128)S(1)} %get-tuple-element.79), channel_id=1, source_target_pairs={{0,1},{1,2},{2,3},{3,4},{4,5},{5,6},{6,7},{8,9},{9,10},{10,11},{11... | collective-permute-start | bytes 196616 | tf_op jit(solution)/shard_map/ppermute | solution.py:19
  505.8 9.0 %collective-permute-done.5 = f32[4,1,32,128]{2,1,0,3:T(1,128)S(1)} collective-permute-done((f32[4,1,32,128]{2,1,0,3:T(1,128)S(1)}, f32[4,1,32,128]{2,1,0,3:T(1,128)S(1)}, u32[]{:S(2)}, u32[]{:S(2)}) %collective-permute-start.5) | collective-permute-done | bytes 65568 | tf_op jit(solution)/shard_map/ppermute | solution.py:19
  514.7 1.1 fusion.3
  516.1 1.0 copy.144
  (89 shorter events, 3.7 us)
Async XLA Ops:
  0.6 23.3 %copy-start = (f32[1,32,128]{2,1,0:T(8,128)S(1)}, f32[1,32,128]{2,1,0:T(8,128)}, u32[]{:S(2)}) copy-start(f32[1,32,128]{2,1,0:T(8,128)} %param.38) | copy-start | bytes 49156
  0.6 0.9 copy-start.13
  1.6 0.8 copy-start.14
  2.4 0.8 copy-start.15
  2.4 0.8 copy-start.23
  4.5 8.9 %copy-start.21 = (f32[1,32,128]{2,1,0:T(8,128)S(1)}, f32[1,32,128]{2,1,0:T(8,128)}, u32[]{:S(2)}) copy-start(f32[1,32,128]{2,1,0:T(8,128)} %param.32) | copy-start | bytes 49156
  4.5 19.0 %all-to-all-start = ((f32[4,32,512]{2,0,1:T(4,128)}), f32[4,32,512]{2,0,1:T(4,128)S(1)}, u32[]{:S(2)}, u32[]{:S(2)}) async-start(f32[4,32,512]{2,0,1:T(4,128)} %pad_maximum_fusion), calls=%async_computation | async-start | bytes 524288 | tf_op jit(solution)/shard_map/all_to_all | solution.py:95
  13.5 0.8 copy-start.20
  14.4 0.8 copy-start.18
  15.1 0.8 copy-start.19
  15.1 0.9 copy-start.11
  15.9 342.6 %copy-start.2 = (f32[2,32,128]{1,0,2:T(2,128)}, f32[2,32,128]{1,0,2:T(2,128)S(1)}, u32[]{:S(2)}) copy-start(f32[2,32,128]{1,0,2:T(2,128)S(1)} %copy.134) | copy-start | bytes 98308
  16.4 0.7 copy-start.25
  17.6 0.7 copy-start.24
  23.9 90.6 %copy-start.1 = (f32[1,32,128]{2,1,0:T(8,128)S(1)}, f32[1,32,128]{2,1,0:T(8,128)}, u32[]{:S(2)}) copy-start(f32[1,32,128]{2,1,0:T(8,128)} %param.37) | copy-start | bytes 49156
  341.0 4.1 copy-start.9
  342.7 2.4 copy-start.16
  343.1 14.6 %collective-permute-start.1 = (f32[4,1,32,128]{2,1,0,3:T(1,128)S(1)}, f32[4,1,32,128]{2,1,0,3:T(1,128)S(1)}, u32[]{:S(2)}, u32[]{:S(2)}) collective-permute-start(f32[4,1,32,128]{2,1,0,3:T(1,128)S(1)} %get-tuple-element.89), channel_id=1, source_target_pairs={{1,0},{2,1},{3,2},{4,3},{5,4},{6,5},{7,6},{9,8},{10,9},{11,10},{12... | collective-permute-start | bytes 196616 | tf_op jit(solution)/shard_map/ppermute | solution.py:19
  357.8 0.7 copy-start.8
  361.5 0.7 copy-start.22
  362.3 2.7 collective-permute-start
  363.0 20.0 %collective-permute-start.2 = (f32[4,1,32,128]{2,1,0,3:T(1,128)S(1)}, f32[4,1,32,128]{2,1,0,3:T(1,128)S(1)}, u32[]{:S(2)}, u32[]{:S(2)}) collective-permute-start(f32[4,1,32,128]{2,1,0,3:T(1,128)S(1)} %get-tuple-element.86), channel_id=1, source_target_pairs={{0,1},{1,2},{2,3},{3,4},{4,5},{5,6},{6,7},{8,9},{9,10},{10,11},{11... | collective-permute-start | bytes 196616 | tf_op jit(solution)/shard_map/ppermute | solution.py:19
  384.4 4.1 copy-start.12
  385.5 19.2 %collective-permute-start.4 = (f32[4,1,32,128]{2,1,0,3:T(1,128)S(1)}, f32[4,1,32,128]{2,1,0,3:T(1,128)S(1)}, u32[]{:S(2)}, u32[]{:S(2)}) collective-permute-start(f32[4,1,32,128]{2,1,0,3:T(1,128)S(1)} %get-tuple-element.82), channel_id=1, source_target_pairs={{1,0},{2,1},{3,2},{4,3},{5,4},{6,5},{7,6},{9,8},{10,9},{11,10},{12... | collective-permute-start | bytes 196616 | tf_op jit(solution)/shard_map/ppermute | solution.py:19
  388.8 16.6 %copy-start.3 = (f32[2,32,128]{1,0,2:T(2,128)S(1)}, f32[2,32,128]{1,0,2:T(2,128)}, u32[]{:S(2)}) copy-start(f32[2,32,128]{1,0,2:T(2,128)} %copy-done.2) | copy-start | bytes 98308
  388.8 16.6 %copy-start.4 = (f32[4,1,32,128]{2,1,0,3:T(1,128)S(1)}, f32[4,1,32,128]{2,1,0,3:T(1,128)}, u32[]{:S(2)}) copy-start(f32[4,1,32,128]{2,1,0,3:T(1,128)} %get-tuple-element.81) | copy-start | bytes 196612
  404.7 0.7 copy-start.7
  409.1 0.8 copy-start.6
  409.2 1.8 copy-start.5
  410.9 94.9 %collective-permute-start.3 = (f32[4,2,32]{2,1,0:T(2,128)S(1)}, f32[4,2,32]{2,1,0:T(2,128)S(1)}, u32[]{:S(2)}, u32[]{:S(2)}) collective-permute-start(f32[4,2,32]{2,1,0:T(2,128)S(1)} %multiply_select_fusion), channel_id=1, source_target_pairs={{0,248},{8,0},{16,8},{24,16},{32,24},{40,32},{48,40},{56,48},{64,5... | collective-permute-start | bytes 3080 | tf_op jit(solution)/shard_map/ppermute | solution.py:13
  498.6 0.8 copy-start.10
  498.6 0.8 copy-start.17
  500.0 14.7 %collective-permute-start.5 = (f32[4,1,32,128]{2,1,0,3:T(1,128)S(1)}, f32[4,1,32,128]{2,1,0,3:T(1,128)S(1)}, u32[]{:S(2)}, u32[]{:S(2)}) collective-permute-start(f32[4,1,32,128]{2,1,0,3:T(1,128)S(1)} %get-tuple-element.79), channel_id=1, source_target_pairs={{0,1},{1,2},{2,3},{3,4},{4,5},{5,6},{6,7},{8,9},{9,10},{10,11},{11... | collective-permute-start | bytes 196616 | tf_op jit(solution)/shard_map/ppermute | solution.py:19
